TPU v7x, 512 devices: a whole 4x4x16 slice. The times are simulated.
512 devices in a mesh: region: 64 (over z, x), split: 8 (over y, core).
Axes of the slice: x: 4, y: 4, z: 16, core: 2. Of those that a mesh axis runs over, the one named last changes fastest.
Arguments:
- vectors: float32 [294912, 256], P(('region', 'split'))
- hessian: bfloat16 [1536, 12, 192, 192], P(('region', 'split')), may hold values from -0.125 to 0.125
- block_cols: int32 [1536, 12], P(('region', 'split')), may hold values from 0 to 35, as said below
- live_blocks: int32 [1536], P(('region', 'split')), may hold values from 6 to 12, as said below
- halo_lists: int32 [64, 2, 6], P('region'), may hold values from 0 to 23, as said below
- bounds: float32 [2], replicated, as said below
Outputs:
- basis: float32 [294912, 256], P(('region', 'split'))
- projected: float32 [256, 256], replicated
Inputs may be any that keep to these rules, and one draw needn't show every extreme that they name: `block_cols`: in each row the entries are distinct and entry 0 is the row's own block within its region; values below 24 name blocks of the row's region, 24 + j the j-th block received from the lower region, 30 + j the j-th from the upper region. `live_blocks`: the first block row of every region has all 12 blocks intact. `halo_lists`: each list holds distinct block indices within the region. bounds[0] < 0 < bounds[1].
All inputs are finite; a program needn't handle non-finite values.
Results may differ from a plain program's by a relative error of at most 0.0005.
The roundings to bfloat16 on the way count: a program that leaves them out, or rounds other values in their place, can miss the bound.
Values may be sent and summed in bfloat16 or wider, within the bound.
A program may use at most 64 MiB of HBM per device.

v0:
```python
import jax
import jax.numpy as jnp
from jax import lax
from jax.sharding import PartitionSpec as P


def shifted(value, axis, steps):
    count = lax.axis_size(axis)
    pairs = [(source, (source + steps) % count) for source in range(count)]
    return lax.ppermute(value, axis, pairs)


def apply_blocks(operand, hessian, block_cols, live_blocks, halo_lists):
    row_blocks = hessian.shape[0]
    block_size = hessian.shape[2]
    mode_count = operand.shape[1]
    shard_blocks = operand.reshape(row_blocks, block_size, mode_count)
    region = lax.all_gather(shard_blocks, "split", axis=0, tiled=True)
    send_lower = region[halo_lists[0, 0]]
    send_upper = region[halo_lists[0, 1]]
    from_lower = shifted(send_upper, "region", 1)
    from_upper = shifted(send_lower, "region", -1)
    candidates = jnp.concatenate([region, from_lower, from_upper], 0)
    picked = candidates[block_cols]
    used_mask = lax.broadcasted_iota(jnp.int32, block_cols.shape, 1) < live_blocks[:, None]
    picked = jnp.where(used_mask[:, :, None, None], picked, jnp.zeros((), jnp.bfloat16))
    product = jnp.einsum("rkij,rkjm->rim", hessian, picked, preferred_element_type=jnp.float32)
    return product.reshape(row_blocks * block_size, mode_count)


def local(vectors, hessian, block_cols, live_blocks, halo_lists, bounds):
    centre = 0.5 * (bounds[0] + bounds[1])
    half_width = 0.5 * (bounds[1] - bounds[0])
    first = apply_blocks(vectors.astype(jnp.bfloat16), hessian, block_cols, live_blocks, halo_lists)
    filtered_one = (first - centre * vectors) / half_width
    second = apply_blocks(
        filtered_one.astype(jnp.bfloat16), hessian, block_cols, live_blocks, halo_lists
    )
    filtered_two = 2.0 * (second - centre * filtered_one) / half_width - vectors
    image = apply_blocks(
        filtered_two.astype(jnp.bfloat16), hessian, block_cols, live_blocks, halo_lists
    )
    total_rows = vectors.shape[0] * lax.axis_size("region") * lax.axis_size("split")
    contract = (((0,), (0,)), ((), ()))
    gram_part = lax.dot_general(
        filtered_two, filtered_two, contract, precision=lax.Precision.HIGHEST
    )
    cross_part = lax.dot_general(filtered_two, image, contract, precision=lax.Precision.HIGHEST)
    gram, cross = lax.psum((gram_part, cross_part), ("region", "split"))
    gram = gram / total_rows
    cross = cross / total_rows
    lower = jnp.linalg.cholesky(gram)
    basis = jax.scipy.linalg.solve_triangular(lower, filtered_two.T, lower=True).T
    partial_left = jax.scipy.linalg.solve_triangular(lower, cross, lower=True)
    projected = jax.scipy.linalg.solve_triangular(lower, partial_left.T, lower=True).T
    return (basis, projected)


def solution(mesh):
    placed = (
        P(("region", "split"), None),
        P(("region", "split"), None, None, None),
        P(("region", "split"), None),
        P(("region", "split")),
        P("region", None, None),
        P(),
    )
    return jax.shard_map(
        local,
        mesh=mesh,
        in_specs=placed,
        out_specs=(P(("region", "split"), None), P()),
        check_vma=False,
    )
```

profile of v0, /device:TPU:1, one launch (start us, length us, event | category | flops | bytes accessed | tf_op | source)
XLA Modules:
  0.0 814.2 jit_solution(8782221556383976657)
XLA Ops:
  7.2 2.0 convert_element_type.9
  10.1 39.6 %all-gather.4.cloned.1.call-done = bf16[24,192,256]{2,1,0:T(8,128)(2,1)} async-done(((bf16[3,192,256]{2,1,0:T(8,128)(2,1)}), bf16[24,192,256]{2,1,0:T(8,128)(2,1)}) %all-gather.4.cloned.1.call-update) | async-done | bytes 2359312 | tf_op jit(solution)/shard_map/all_gather | solution.py:18
  49.7 3.1 gather_fusion
  52.8 3.1 collective-permute-start
  55.9 3.1 gather_fusion.1
  59.0 6.6 collective-permute-start.1
  69.7 4.6 collective-permute-done
  74.3 4.0 collective-permute-done.1
  78.3 3.4 pad_maximum_fusion
  81.7 4.8 gather_fusion.2
  86.6 3.0 fusion.4
  90.6 34.4 %all-gather.6.cloned.1.call-done = bf16[24,192,256]{2,1,0:T(8,128)(2,1)} async-done(((bf16[3,192,256]{2,1,0:T(8,128)(2,1)}), bf16[24,192,256]{2,1,0:T(8,128)(2,1)}) %all-gather.6.cloned.1.call-update) | async-done | bytes 2359312 | tf_op jit(solution)/shard_map/all_gather | solution.py:18
  125.0 3.1 gather_fusion.3
  128.1 3.1 collective-permute-start.2
  131.2 3.1 gather_fusion.4
  134.3 6.6 collective-permute-start.3
  141.0 8.7 %collective-permute-done.2 = bf16[6,192,256]{2,1,0:T(8,128)(2,1)} collective-permute-done((bf16[6,192,256]{2,1,0:T(8,128)(2,1)}, bf16[6,192,256]{2,1,0:T(8,128)(2,1)}, u32[]{:S(2)}, u32[]{:S(2)}) %collective-permute-start.2) | collective-permute-done | bytes 589856 | tf_op jit(solution)/shard_map/ppermute | solution.py:10
  149.7 4.0 collective-permute-done.3
  153.7 3.3 pad_maximum_fusion.1
  157.0 4.8 gather_fusion.5
  161.9 3.1 fusion.2
  166.1 34.3 %all-gather.8.cloned.1.call-done = bf16[24,192,256]{2,1,0:T(8,128)(2,1)} async-done(((bf16[3,192,256]{2,1,0:T(8,128)(2,1)}), bf16[24,192,256]{2,1,0:T(8,128)(2,1)}) %all-gather.8.cloned.1.call-update) | async-done | bytes 2359312 | tf_op jit(solution)/shard_map/all_gather | solution.py:18
  200.5 3.1 gather_fusion.6
  203.6 3.1 collective-permute-start.4
  206.7 3.1 gather_fusion.7
  209.8 6.6 collective-permute-start.5
  216.4 3.2 fusion.42
  219.6 5.5 collective-permute-done.4
  225.1 4.0 collective-permute-done.5
  229.1 3.3 pad_maximum_fusion.2
  232.5 4.8 gather_fusion.8
  237.3 3.0 fusion
  240.3 1.9 fusion.43
  242.3 466.4 %all-reduce.4.cloned.1.call-done = (f32[256,256]{0,1:T(8,128)}, f32[256,256]{0,1:T(8,128)}) async-done(((f32[256,256]{0,1:T(8,128)}, f32[256,256]{0,1:T(8,128)}), (f32[256,256]{0,1:T(8,128)}, f32[256,256]{0,1:T(8,128)})) %all-reduce.4.cloned.1.call-update) | async-done | bytes 524304 | tf_op jit(solution)/shard_map/psum | solution.py:49
  708.8 1.9 broadcast_multiply_fusion
  710.6 1.8 copy.13
  714.8 13.2 %cholesky.50 = f32[128,128]{1,0:T(8,128)} custom-call(f32[128,128]{1,0:T(8,128)} %cholesky.118), custom_call_target="Cholesky" | custom-call | tf_op jit(solution)/shard_map/jit(cholesky)/cholesky | solution.py:52
  729.5 1.6 cholesky.113
  731.0 11.3 %custom-call.18 = f32[1,128,128]{1,2,0:T(8,128)} custom-call(f32[1,128,128]{2,1,0:T(8,128)} %get-tuple-element.48), custom_call_target="InvertDiagBlocksLowerTriangular" | custom-call | tf_op jit(solution)/shard_map/jit(cholesky)/cholesky | solution.py:52
  742.3 1.7 constant_dynamic-update-slice_fusion.1
  744.0 1.7 convolution_subtract_fusion.3
  745.7 13.4 %cholesky.105 = f32[128,128]{1,0:T(8,128)} custom-call(f32[128,128]{1,0:T(8,128)} %convolution_subtract_fusion.3), custom_call_target="Cholesky" | custom-call | tf_op jit(solution)/shard_map/jit(cholesky)/cholesky | solution.py:52
  763.2 1.7 select_select_fusion
  765.0 6.9 while.5
  765.6 2.9 bitcast_dynamic-update-slice_fusion.2
  769.0 2.8 bitcast_dynamic-update-slice_fusion.2
  771.8 21.1 %custom-call.19 = f32[2,128,128]{1,2,0:T(8,128)} custom-call(f32[2,128,128]{2,1,0:T(8,128)} %get-tuple-element.18), custom_call_target="InvertDiagBlocksLowerTriangular" | custom-call | tf_op jit(solution)/shard_map/jit(_solve_triangular)/triangular_solve | solution.py:53
  801.0 1.8 copy.15
  (61 shorter events, 25.4 us)
Async XLA Ops:
  7.2 79.4 %copy-start = (bf16[3,12,192,192]{3,2,1,0:T(8,128)(2,1)S(1)}, bf16[3,12,192,192]{3,2,1,0:T(8,128)(2,1)}, u32[]{:S(2)}) copy-start(bf16[3,12,192,192]{3,2,1,0:T(8,128)(2,1)} %param.9) | copy-start | bytes 7962628
  7.2 58.4 %copy-start.8 = (f32[2]{0:T(128)S(1)}, f32[2]{0:T(128)}, u32[]{:S(2)}) copy-start(f32[2]{0:T(128)} %param.13) | copy-start | bytes 28
  7.2 61.7 %copy-start.7 = (s32[3,12]{1,0:T(4,128)S(1)}, s32[3,12]{1,0:T(4,128)}, u32[]{:S(2)}) copy-start(s32[3,12]{1,0:T(4,128)} %param.10) | copy-start | bytes 436
  7.2 42.5 %all-gather.4.cloned.1.call-start = ((), (), s32[]{:S(2)}) async-start(), calls=%async_computation | async-start | bytes 2654208 | tf_op jit(solution)/shard_map/all_gather | solution.py:18
  9.2 115.8 %all-gather.6.cloned.1.call-start = ((), (), s32[]{:S(2)}) async-start(), calls=%async_computation.1 | async-start | bytes 2654208 | tf_op jit(solution)/shard_map/all_gather | solution.py:18
  52.8 21.5 %collective-permute-start = (bf16[6,192,256]{2,1,0:T(8,128)(2,1)}, bf16[6,192,256]{2,1,0:T(8,128)(2,1)}, u32[]{:S(2)}, u32[]{:S(2)}) collective-permute-start(bf16[6,192,256]{2,1,0:T(8,128)(2,1)} %gather_fusion), channel_id=1, source_target_pairs={{0,8},{8,16},{16,24},{24,32},{32,40},{40,48},{48,56},{56,64},{64,7... | collective-permute-start | bytes 1769480 | tf_op jit(solution)/shard_map/ppermute | solution.py:10
  59.0 19.3 %collective-permute-start.1 = (bf16[6,192,256]{2,1,0:T(8,128)(2,1)}, bf16[6,192,256]{2,1,0:T(8,128)(2,1)}, u32[]{:S(2)}, u32[]{:S(2)}) collective-permute-start(bf16[6,192,256]{2,1,0:T(8,128)(2,1)} %gather_fusion.1), channel_id=1, source_target_pairs={{0,504},{8,0},{16,8},{24,16},{32,24},{40,32},{48,40},{56,48},{64,5... | collective-permute-start | bytes 1769480 | tf_op jit(solution)/shard_map/ppermute | solution.py:10
  86.6 3.1 copy-start.2
  89.6 0.9 copy-start.4
  90.6 109.9 %all-gather.8.cloned.1.call-start = ((), (), s32[]{:S(2)}) async-start(), calls=%async_computation.2 | async-start | bytes 2654208 | tf_op jit(solution)/shard_map/all_gather | solution.py:18
  128.1 21.5 %collective-permute-start.2 = (bf16[6,192,256]{2,1,0:T(8,128)(2,1)}, bf16[6,192,256]{2,1,0:T(8,128)(2,1)}, u32[]{:S(2)}, u32[]{:S(2)}) collective-permute-start(bf16[6,192,256]{2,1,0:T(8,128)(2,1)} %gather_fusion.3), channel_id=1, source_target_pairs={{0,8},{8,16},{16,24},{24,32},{32,40},{40,48},{48,56},{56,64},{64,7... | collective-permute-start | bytes 1769480 | tf_op jit(solution)/shard_map/ppermute | solution.py:10
  134.3 19.3 %collective-permute-start.3 = (bf16[6,192,256]{2,1,0:T(8,128)(2,1)}, bf16[6,192,256]{2,1,0:T(8,128)(2,1)S(1)}, u32[]{:S(2)}, u32[]{:S(2)}) collective-permute-start(bf16[6,192,256]{2,1,0:T(8,128)(2,1)} %gather_fusion.4), channel_id=1, source_target_pairs={{0,504},{8,0},{16,8},{24,16},{32,24},{40,32},{48,40},{56,48},{64,5... | collective-permute-start | bytes 1769480 | tf_op jit(solution)/shard_map/ppermute | solution.py:10
  161.9 3.1 copy-start.3
  161.9 3.1 copy-start.5
  166.1 542.7 %all-reduce.4.cloned.1.call-start = ((), (), s32[]{:S(2)}) async-start(), calls=%async_computation.3 | async-start | bytes 1048576 | tf_op jit(solution)/shard_map/psum | solution.py:49
  203.6 21.5 %collective-permute-start.4 = (bf16[6,192,256]{2,1,0:T(8,128)(2,1)}, bf16[6,192,256]{2,1,0:T(8,128)(2,1)}, u32[]{:S(2)}, u32[]{:S(2)}) collective-permute-start(bf16[6,192,256]{2,1,0:T(8,128)(2,1)} %gather_fusion.6), channel_id=1, source_target_pairs={{0,8},{8,16},{16,24},{24,32},{32,40},{40,48},{48,56},{56,64},{64,7... | collective-permute-start | bytes 1769480 | tf_op jit(solution)/shard_map/ppermute | solution.py:10
  209.8 19.3 %collective-permute-start.5 = (bf16[6,192,256]{2,1,0:T(8,128)(2,1)}, bf16[6,192,256]{2,1,0:T(8,128)(2,1)S(1)}, u32[]{:S(2)}, u32[]{:S(2)}) collective-permute-start(bf16[6,192,256]{2,1,0:T(8,128)(2,1)} %gather_fusion.7), channel_id=1, source_target_pairs={{0,504},{8,0},{16,8},{24,16},{32,24},{40,32},{48,40},{56,48},{64,5... | collective-permute-start | bytes 1769480 | tf_op jit(solution)/shard_map/ppermute | solution.py:10
  237.3 3.0 copy-start.1
  713.5 0.7 copy-start.6
Sparse Core Ops, SparseCore 0:
  10.7 38.9 all-gather.3
  90.7 34.3 all-gather.5
  166.2 34.2 all-gather.7
  242.4 466.3 all-reduce.3
where the time goes:
time: 816 us; the launch traced here: 814 us
  waiting for transfers between devices  606 us (74%)
  other arithmetic  85.1 us (10%)
  local copies, waits for them, and re-layouts  47.2 us (6%)
  starting transfers between devices  29.3 us (4%)
  matrix products  29 us (4%)
  between operations  18 us (2%)
    psum x1, waiting for transfers between devices, local(): gram, cross = lax.psum((gram_part, cross_part), ('region', 'split'))  466 us
    all_gather x3, waiting for transfers between devices, apply_blocks(): region = lax.all_gather(shard_blocks, 'split', axis=0, tiled=True)  108 us
    another operation x7, other arithmetic, local(): lower = jnp.linalg.cholesky(gram)  42.1 us
    ppermute x6, waiting for transfers between devices, shifted(): return lax.ppermute(value, axis, pairs)  30.8 us
    ppermute x6, starting transfers between devices, shifted(): return lax.ppermute(value, axis, pairs)  29.1 us
    another operation x3, other arithmetic, local(): jax.scipy.linalg.solve_triangular(lower, filtered_two.T, lower=True)  22.8 us
  transfers between devices with their start and end apart: 10, of which 10 were waited for; matrix products, arithmetic and copies ran while one was open for 2% of the time, Pallas kernels for 0%

commit v1 on v0

--- a/solution.py
+++ b/solution.py
@@ -15,7 +15,9 @@
     block_size = hessian.shape[2]
     mode_count = operand.shape[1]
     shard_blocks = operand.reshape(row_blocks, block_size, mode_count)
-    region = lax.all_gather(shard_blocks, "split", axis=0, tiled=True)
+    region = jnp.concatenate(
+        lax.all_to_all(jnp.stack([shard_blocks] * lax.axis_size("split")), "split", 0, 0), axis=0
+    )
     send_lower = region[halo_lists[0, 0]]
     send_upper = region[halo_lists[0, 1]]
     from_lower = shifted(send_upper, "region", 1)

time: 816 us -> 810 us (level)
  waiting for transfers between devices: 606 us -> 521 us
  blocking collectives: 0 us -> 68 us
  starting transfers between devices: 29.3 us -> 39.8 us
    all_gather x3 -> x0, waiting for transfers between devices: 108 us -> none  [apply_blocks(): region = lax.all_gather(shard_blocks, 'split', axis=0, tiled=True)]
    all_to_all x0 -> x2, blocking collectives: none -> 68 us  [apply_blocks(): lax.all_to_all(jnp.stack([shard_blocks] * lax.axis_size('split')), 'split...]
    all_to_all x0 -> x1, waiting for transfers between devices: none -> 29.1 us  [apply_blocks(): lax.all_to_all(jnp.stack([shard_blocks] * lax.axis_size('split')), 'split...]
    all_to_all x0 -> x1, starting transfers between devices: none -> 11.2 us  [apply_blocks(): lax.all_to_all(jnp.stack([shard_blocks] * lax.axis_size('split')), 'split...]
  transfers between devices with their start and end apart: 10 -> 8, of which waited for: 10 -> 8; matrix products, arithmetic and copies ran while one was open for 2% -> 1% of each run, Pallas kernels for 0% -> 0%
where the time goes in v1:
time: 810 us; the launch traced here: 808 us
  waiting for transfers between devices  521 us (64%)
  other arithmetic  82.5 us (10%)
  blocking collectives  68 us (8%)
  local copies, waits for them, and re-layouts  49.4 us (6%)
  starting transfers between devices  39.8 us (5%)
  matrix products  29.1 us (4%)
  between operations  18 us (2%)
    psum x1, waiting for transfers between devices, local(): gram, cross = lax.psum((gram_part, cross_part), ('region', 'split'))  464 us
    all_to_all x2, blocking collectives, apply_blocks(): lax.all_to_all(jnp.stack([shard_blocks] * lax.axis_size('split')), 'split...  68 us
    another operation x7, other arithmetic, local(): lower = jnp.linalg.cholesky(gram)  42.1 us
    all_to_all x1, waiting for transfers between devices, apply_blocks(): lax.all_to_all(jnp.stack([shard_blocks] * lax.axis_size('split')), 'split...  29.1 us
    ppermute x6, waiting for transfers between devices, shifted(): return lax.ppermute(value, axis, pairs)  28.8 us
    ppermute x6, starting transfers between devices, shifted(): return lax.ppermute(value, axis, pairs)  28.6 us
    another operation x3, other arithmetic, local(): jax.scipy.linalg.solve_triangular(lower, filtered_two.T, lower=True)  22.8 us
  transfers between devices with their start and end apart: 8, of which 8 were waited for; matrix products, arithmetic and copies ran while one was open for 1% of the time, Pallas kernels for 0%

profile of v1, /device:TPU:1, one launch (start us, length us, event | category | flops | bytes accessed | tf_op | source)
XLA Modules:
  0.0 808.3 jit_solution(3798709986296327275)
XLA Ops:
  8.4 1.7 stack.9
  10.1 11.2 %all-to-all-start = ((bf16[8,3,192,256]{3,2,1,0:T(8,128)(2,1)}), bf16[8,3,192,256]{3,2,1,0:T(8,128)(2,1)}, u32[]{:S(2)}, u32[]{:S(2)}) async-start(bf16[8,3,192,256]{3,2,1,0:T(8,128)(2,1)} %stack.9), calls=%async_computation | async-start | bytes 4718592 | tf_op jit(solution)/shard_map/all_to_all | solution.py:19
  21.4 29.1 %all-to-all-done = bf16[8,3,192,256]{3,2,1,0:T(8,128)(2,1)} async-done(((bf16[8,3,192,256]{3,2,1,0:T(8,128)(2,1)}), bf16[8,3,192,256]{3,2,1,0:T(8,128)(2,1)}, u32[]{:S(2)}, u32[]{:S(2)}) %all-to-all-start) | async-done | bytes 2359328 | tf_op jit(solution)/shard_map/all_to_all | solution.py:19
  50.5 3.1 gather_fusion
  53.6 1.9 collective-permute-start
  55.5 3.1 gather_fusion.1
  58.6 8.1 %collective-permute-start.1 = (bf16[6,192,256]{2,1,0:T(8,128)(2,1)}, bf16[6,192,256]{2,1,0:T(8,128)(2,1)}, u32[]{:S(2)}, u32[]{:S(2)}) collective-permute-start(bf16[6,192,256]{2,1,0:T(8,128)(2,1)} %gather_fusion.1), channel_id=1, source_target_pairs={{0,504},{8,0},{16,8},{24,16},{32,24},{40,32},{48,40},{56,48},{64,5... | collective-permute-start | bytes 1769480 | tf_op jit(solution)/shard_map/ppermute | solution.py:10
  70.6 4.2 collective-permute-done
  74.8 4.0 collective-permute-done.1
  78.8 3.5 pad_maximum_fusion
  82.2 4.8 gather_fusion.2
  87.1 3.0 fusion.4
  90.5 34.0 %all_to_all.15 = bf16[8,3,192,256]{3,2,1,0:T(8,128)(2,1)} all-to-all(bf16[8,3,192,256]{3,2,1,0:T(8,128)(2,1)S(1)} %stack.10), channel_id=1, replica_groups=mesh['region'=64,'split'=8] {'split'}, dimensions={0} | all-to-all | bytes 4718592 | tf_op jit(solution)/shard_map/all_to_all | solution.py:19
  124.5 3.1 gather_fusion.3
  127.5 3.1 gather_fusion.4
  130.6 1.9 collective-permute-start.2
  132.6 7.4 collective-permute-start.3
  140.0 10.9 %collective-permute-done.2 = bf16[6,192,256]{2,1,0:T(8,128)(2,1)S(1)} collective-permute-done((bf16[6,192,256]{2,1,0:T(8,128)(2,1)}, bf16[6,192,256]{2,1,0:T(8,128)(2,1)S(1)}, u32[]{:S(2)}, u32[]{:S(2)}) %collective-permute-start.2) | collective-permute-done | bytes 589856 | tf_op jit(solution)/shard_map/ppermute | solution.py:10
  151.9 3.3 pad_maximum_fusion.1
  155.2 4.8 gather_fusion.5
  160.0 3.1 fusion.2
  164.4 34.1 %all_to_all.16 = bf16[8,3,192,256]{3,2,1,0:T(8,128)(2,1)} all-to-all(bf16[8,3,192,256]{3,2,1,0:T(8,128)(2,1)S(1)} %stack.11), channel_id=1, replica_groups=mesh['region'=64,'split'=8] {'split'}, dimensions={0} | all-to-all | bytes 4718592 | tf_op jit(solution)/shard_map/all_to_all | solution.py:19
  198.5 3.1 gather_fusion.6
  201.6 3.1 gather_fusion.7
  204.6 1.9 collective-permute-start.4
  206.6 7.3 collective-permute-start.5
  213.9 3.3 fusion.42
  217.2 7.7 collective-permute-done.4
  225.8 3.3 pad_maximum_fusion.2
  229.1 4.8 gather_fusion.8
  233.9 3.0 fusion
  237.0 2.0 fusion.43
  239.0 463.5 %all-reduce.4.cloned.1.call-done = (f32[256,256]{0,1:T(8,128)}, f32[256,256]{0,1:T(8,128)}) async-done(((f32[256,256]{0,1:T(8,128)}, f32[256,256]{0,1:T(8,128)}), (f32[256,256]{0,1:T(8,128)}, f32[256,256]{0,1:T(8,128)})) %all-reduce.4.cloned.1.call-update) | async-done | bytes 524304 | tf_op jit(solution)/shard_map/psum | solution.py:51
  702.5 1.9 broadcast_multiply_fusion
  704.4 1.8 copy.9
  708.5 13.2 %cholesky.50 = f32[128,128]{1,0:T(8,128)} custom-call(f32[128,128]{1,0:T(8,128)} %cholesky.118), custom_call_target="Cholesky" | custom-call | tf_op jit(solution)/shard_map/jit(cholesky)/cholesky | solution.py:54
  723.2 1.5 cholesky.113
  724.7 11.3 %custom-call.18 = f32[1,128,128]{1,2,0:T(8,128)} custom-call(f32[1,128,128]{2,1,0:T(8,128)} %get-tuple-element.46), custom_call_target="InvertDiagBlocksLowerTriangular" | custom-call | tf_op jit(solution)/shard_map/jit(cholesky)/cholesky | solution.py:54
  736.0 1.7 constant_dynamic-update-slice_fusion.1
  737.7 1.7 convolution_subtract_fusion.3
  739.4 13.4 %cholesky.105 = f32[128,128]{1,0:T(8,128)} custom-call(f32[128,128]{1,0:T(8,128)} %convolution_subtract_fusion.3), custom_call_target="Cholesky" | custom-call | tf_op jit(solution)/shard_map/jit(cholesky)/cholesky | solution.py:54
  752.8 1.5 select_reduce_fusion
  756.8 1.7 select_select_fusion
  758.6 7.0 while.5
  759.2 2.9 bitcast_dynamic-update-slice_fusion.2
  762.8 2.8 bitcast_dynamic-update-slice_fusion.2
  765.6 21.1 %custom-call.19 = f32[2,128,128]{1,2,0:T(8,128)} custom-call(f32[2,128,128]{2,1,0:T(8,128)} %get-tuple-element.18), custom_call_target="InvertDiagBlocksLowerTriangular" | custom-call | tf_op jit(solution)/shard_map/jit(_solve_triangular)/triangular_solve | solution.py:55
  794.7 1.8 copy.11
  (61 shorter events, 25.8 us)
Async XLA Ops:
  7.2 79.9 %copy-start = (bf16[3,12,192,192]{3,2,1,0:T(8,128)(2,1)S(1)}, bf16[3,12,192,192]{3,2,1,0:T(8,128)(2,1)}, u32[]{:S(2)}) copy-start(bf16[3,12,192,192]{3,2,1,0:T(8,128)(2,1)} %param.9) | copy-start | bytes 7962628
  8.4 12.9 %copy-start.9 = (s32[1,2,6]{2,1,0:T(2,128)S(1)}, s32[1,2,6]{2,1,0:T(2,128)}, u32[]{:S(2)}) copy-start(s32[1,2,6]{2,1,0:T(2,128)} %param.12) | copy-start | bytes 148
  10.1 56.6 %copy-start.8 = (f32[2]{0:T(128)S(1)}, f32[2]{0:T(128)}, u32[]{:S(2)}) copy-start(f32[2]{0:T(128)} %param.13) | copy-start | bytes 28
  10.1 59.6 %copy-start.7 = (s32[3,12]{1,0:T(4,128)S(1)}, s32[3,12]{1,0:T(4,128)}, u32[]{:S(2)}) copy-start(s32[3,12]{1,0:T(4,128)} %param.10) | copy-start | bytes 436
  10.1 40.4 %all-to-all-start = ((bf16[8,3,192,256]{3,2,1,0:T(8,128)(2,1)}), bf16[8,3,192,256]{3,2,1,0:T(8,128)(2,1)}, u32[]{:S(2)}, u32[]{:S(2)}) async-start(bf16[8,3,192,256]{3,2,1,0:T(8,128)(2,1)} %stack.9), calls=%async_computation | async-start | bytes 4718592 | tf_op jit(solution)/shard_map/all_to_all | solution.py:19
  21.4 681.1 %all-reduce.4.cloned.1.call-start = ((), (), s32[]{:S(2)}) async-start(), calls=%async_computation.3 | async-start | bytes 1048576 | tf_op jit(solution)/shard_map/psum | solution.py:51
  53.6 21.2 %collective-permute-start = (bf16[6,192,256]{2,1,0:T(8,128)(2,1)}, bf16[6,192,256]{2,1,0:T(8,128)(2,1)}, u32[]{:S(2)}, u32[]{:S(2)}) collective-permute-start(bf16[6,192,256]{2,1,0:T(8,128)(2,1)} %gather_fusion), channel_id=1, source_target_pairs={{0,8},{8,16},{16,24},{24,32},{32,40},{40,48},{48,56},{56,64},{64,7... | collective-permute-start | bytes 1769480 | tf_op jit(solution)/shard_map/ppermute | solution.py:10
  58.6 20.2 %collective-permute-start.1 = (bf16[6,192,256]{2,1,0:T(8,128)(2,1)}, bf16[6,192,256]{2,1,0:T(8,128)(2,1)}, u32[]{:S(2)}, u32[]{:S(2)}) collective-permute-start(bf16[6,192,256]{2,1,0:T(8,128)(2,1)} %gather_fusion.1), channel_id=1, source_target_pairs={{0,504},{8,0},{16,8},{24,16},{32,24},{40,32},{48,40},{56,48},{64,5... | collective-permute-start | bytes 1769480 | tf_op jit(solution)/shard_map/ppermute | solution.py:10
  87.1 3.1 copy-start.2
  90.1 34.4 %copy-start.4 = (f32[3,256,192,1]{1,2,3,0:T(8,128)}, f32[3,256,192,1]{1,2,3,0:T(8,128)S(1)}, u32[]{:S(2)}) copy-start(f32[3,256,192,1]{1,2,3,0:T(8,128)S(1)} %fusion.4) | copy-start | bytes 1769476
  130.6 20.3 %collective-permute-start.2 = (bf16[6,192,256]{2,1,0:T(8,128)(2,1)}, bf16[6,192,256]{2,1,0:T(8,128)(2,1)S(1)}, u32[]{:S(2)}, u32[]{:S(2)}) collective-permute-start(bf16[6,192,256]{2,1,0:T(8,128)(2,1)} %gather_fusion.3), channel_id=1, source_target_pairs={{0,8},{8,16},{16,24},{24,32},{32,40},{40,48},{48,56},{56,64},{64,7... | collective-permute-start | bytes 1769480 | tf_op jit(solution)/shard_map/ppermute | solution.py:10
  132.6 19.4 %collective-permute-start.3 = (bf16[6,192,256]{2,1,0:T(8,128)(2,1)}, bf16[6,192,256]{2,1,0:T(8,128)(2,1)S(1)}, u32[]{:S(2)}, u32[]{:S(2)}) collective-permute-start(bf16[6,192,256]{2,1,0:T(8,128)(2,1)} %gather_fusion.4), channel_id=1, source_target_pairs={{0,504},{8,0},{16,8},{24,16},{32,24},{40,32},{48,40},{56,48},{64,5... | collective-permute-start | bytes 1769480 | tf_op jit(solution)/shard_map/ppermute | solution.py:10
  160.0 3.1 copy-start.3
  160.0 3.1 copy-start.5
  204.6 20.2 %collective-permute-start.4 = (bf16[6,192,256]{2,1,0:T(8,128)(2,1)}, bf16[6,192,256]{2,1,0:T(8,128)(2,1)S(1)}, u32[]{:S(2)}, u32[]{:S(2)}) collective-permute-start(bf16[6,192,256]{2,1,0:T(8,128)(2,1)} %gather_fusion.6), channel_id=1, source_target_pairs={{0,8},{8,16},{16,24},{24,32},{32,40},{40,48},{48,56},{56,64},{64,7... | collective-permute-start | bytes 1769480 | tf_op jit(solution)/shard_map/ppermute | solution.py:10
  206.6 19.3 %collective-permute-start.5 = (bf16[6,192,256]{2,1,0:T(8,128)(2,1)}, bf16[6,192,256]{2,1,0:T(8,128)(2,1)S(1)}, u32[]{:S(2)}, u32[]{:S(2)}) collective-permute-start(bf16[6,192,256]{2,1,0:T(8,128)(2,1)} %gather_fusion.7), channel_id=1, source_target_pairs={{0,504},{8,0},{16,8},{24,16},{32,24},{40,32},{48,40},{56,48},{64,5... | collective-permute-start | bytes 1769480 | tf_op jit(solution)/shard_map/ppermute | solution.py:10
  233.9 3.0 copy-start.1
  707.2 0.7 copy-start.6
Sparse Core Ops, SparseCore 0:
  239.1 463.3 all-reduce.3
